TPU v7x, 32 devices: a whole 2x2x4 slice. The times are simulated.
32 devices in a mesh: groups: 2 (over y), inner: 4 (over z), outer: 4 (over x, core).
Axes of the slice: x: 2, y: 2, z: 4, core: 2. Of those that a mesh axis runs over, the one named last changes fastest.
Arguments:
- queries: bfloat16 [8192, 1024], P(('groups', 'outer', 'inner')), parts along dimension 0, may hold values from -6 to 6
- keys: bfloat16 [8192, 1024], P(('groups', 'outer', 'inner')), parts along dimension 0, may hold values from -6 to 6
- values: bfloat16 [8192, 1024], P(('groups', 'outer', 'inner')), parts along dimension 0, may hold values from -6 to 6
- retain: float32 [8192, 8], P(('groups', 'outer', 'inner')), parts along dimension 0, may hold values from 0.4 to 1
- step: float32 [8192, 8], P(('groups', 'outer', 'inner')), parts along dimension 0, may hold values from 0.000625 to 0.0125
- momentum: float32 [8192, 8], P(('groups', 'outer', 'inner')), parts along dimension 0, may hold values from 0.97 to 0.99
- init_memory: float32 [8, 128, 128], replicated, may hold values from -0.1875 to 0.1875
- init_momentum: float32 [8, 128, 128], replicated, may hold values from -0.1875 to 0.1875
Outputs:
- retrieved: bfloat16 [8192, 1024], P(('groups', 'outer', 'inner')), parts along dimension 0
There are 2 independent parts, one for each index of `groups`. A program takes and returns all parts, laid end to end along the dimension named above; an argument that names none is the same for every part. Nothing has to cross between parts.
All inputs are finite; a program needn't handle non-finite values.
Results may differ from a plain program's by a relative error of at most 0.001.
Values sent between devices are 32-bit elements; how exact they have to be, the bound alone decides.
No kernel may reach another device: no remote copies, remote signals or barrier semaphores. Data moves between devices by JAX's collectives and lax.ppermute only.
A program may use at most 256 MiB of HBM per device.

v0:
```python
import jax
import jax.numpy as jnp
from jax import lax
from jax.sharding import PartitionSpec as P


def carried_in(value, axis, join, neutral):
    count, mine = (lax.axis_size(axis), lax.axis_index(axis))
    pieces = jax.tree.map(lambda part: lax.all_gather(part, axis), value)
    total = jax.tree.map(
        lambda part, zero: jnp.full_like(part, 0) + jnp.asarray(zero, part.dtype), value, neutral
    )

    def turn(position, total):
        longer = join(total, jax.tree.map(lambda part: part[position], pieces))
        return jax.tree.map(lambda new, old: jnp.where(position < mine, new, old), longer, total)

    return lax.fori_loop(0, count - 1, turn, total)


def from_root(block, axis, owner):
    block = jnp.where(lax.axis_index(axis) == owner, block, jnp.zeros_like(block))
    return lax.psum(block, axis)


def unit_rows(source, heads):
    rows = source.astype(jnp.float32).reshape(source.shape[0], heads, -1)
    return rows * lax.rsqrt(jnp.sum(rows * rows, -1, keepdims=True) + 1e-06)


def block_terms(queries, keys, values, retain, step, momentum):
    length = queries.shape[0]
    heads = retain.shape[1]
    precise = lax.Precision.HIGHEST
    query_unit = unit_rows(queries, heads)
    key_unit = unit_rows(keys, heads)
    value_rows = values.astype(jnp.float32).reshape(length, heads, -1)
    key_width = key_unit.shape[2]
    log_retain = jnp.cumsum(jnp.log(retain), 0).T
    log_moment = jnp.cumsum(jnp.log(momentum), 0).T
    position = jnp.arange(length)
    causal = (position[:, None] >= position[None, :])[None]
    retain_decay = jnp.where(
        causal,
        jnp.exp(jnp.where(causal, log_retain[:, :, None] - log_retain[:, None, :], 0.0)),
        0.0,
    )
    momentum_decay = jnp.where(
        causal,
        jnp.exp(jnp.where(causal, log_moment[:, :, None] - log_moment[:, None, :], 0.0)),
        0.0,
    )
    weights = jnp.einsum("htu,hur->htr", retain_decay, momentum_decay, precision=precise)
    carry_scale = jnp.einsum("htu,hu->ht", retain_decay, jnp.exp(log_moment), precision=precise)
    scores = jnp.einsum("thd,rhd->htr", query_unit, key_unit, precision=precise)
    step_rows = step.T
    mixing = scores * weights * step_rows[:, None, :]
    memory_weight = weights[:, -1, :] * step_rows
    moment_weight = jnp.exp(log_moment[:, -1:] - log_moment) * step_rows
    memory_gram = jnp.einsum(
        "rhd,hr,rhe->hde", key_unit, memory_weight, key_unit, precision=precise
    )
    moment_gram = jnp.einsum(
        "rhd,hr,rhe->hde", key_unit, moment_weight, key_unit, precision=precise
    )
    identity = jnp.eye(key_width, dtype=jnp.float32)[None]
    retain_end = jnp.exp(log_retain[:, -1])[:, None, None]
    moment_end = jnp.exp(log_moment[:, -1])[:, None, None]
    carry_end = carry_scale[:, -1][:, None, None]
    upper_rows = jnp.concatenate([retain_end * identity - memory_gram, -moment_gram], axis=2)
    lower_rows = jnp.concatenate([carry_end * identity, moment_end * identity], axis=2)
    transition = jnp.concatenate([upper_rows, lower_rows], axis=1)
    memory_write = jnp.einsum(
        "rhd,hr,rhe->hde", value_rows, memory_weight, key_unit, precision=precise
    )
    moment_write = jnp.einsum(
        "rhd,hr,rhe->hde", value_rows, moment_weight, key_unit, precision=precise
    )
    offset = jnp.concatenate([memory_write, moment_write], axis=2)
    local_terms = (query_unit, key_unit, value_rows, jnp.exp(log_retain), carry_scale, mixing)
    return (transition, offset, local_terms)


def block_output(carried, local_terms):
    query_unit, key_unit, value_rows, retain_scale, carry_scale, mixing = local_terms
    precise = lax.Precision.HIGHEST
    key_width = query_unit.shape[2]
    memory = carried[:, :, :key_width]
    moment_part = carried[:, :, key_width:]
    residual = jnp.einsum("rhd,hed->hre", key_unit, memory, precision=precise) - jnp.transpose(
        value_rows, (1, 0, 2)
    )
    result = retain_scale[:, :, None] * jnp.einsum(
        "thd,hed->hte", query_unit, memory, precision=precise
    )
    result = result + carry_scale[:, :, None] * jnp.einsum(
        "thd,hed->hte", query_unit, moment_part, precision=precise
    )
    result = result - jnp.einsum("htr,hre->hte", mixing, residual, precision=precise)
    return jnp.transpose(result, (1, 0, 2)).reshape(query_unit.shape[0], -1).astype(jnp.bfloat16)


def advance_state(carried, transition, offset):
    return jnp.einsum("hij,hjk->hik", carried, transition, precision=lax.Precision.HIGHEST) + offset


def compose(earlier, later):
    joined = jnp.einsum("hij,hjk->hik", earlier[0], later[0], precision=lax.Precision.HIGHEST)
    return (joined, advance_state(earlier[1], later[0], later[1]))


def apply_earlier(gathered, first_state):
    my_group = lax.axis_index("outer")

    def advance_group(index, carried):
        moved = advance_state(carried, gathered[0][index], gathered[1][index])
        return jnp.where(index < my_group, moved, carried)

    return lax.fori_loop(0, gathered[0].shape[0], advance_group, first_state)


def local(queries, keys, values, retain, step, momentum, init_memory, init_momentum):
    transition, offset, local_terms = block_terms(queries, keys, values, retain, step, momentum)
    identity_maps = (
        jnp.broadcast_to(jnp.eye(transition.shape[1], dtype=jnp.float32), transition.shape),
        jnp.zeros_like(offset),
    )
    before = carried_in((transition, offset), "inner", compose, identity_maps)
    through = compose(before, (transition, offset))
    first_state = jnp.concatenate([init_memory, init_momentum], axis=2)
    last_inner = lax.axis_size("inner") - 1
    group_map = (
        from_root(through[0], "inner", last_inner),
        from_root(through[1], "inner", last_inner),
    )
    gathered = (
        lax.all_gather(group_map[0][None], "outer", axis=0, tiled=True),
        lax.all_gather(group_map[1][None], "outer", axis=0, tiled=True),
    )
    entry_state = apply_earlier(gathered, first_state)
    block_state = advance_state(entry_state, before[0], before[1])
    return block_output(block_state, local_terms)


def solution(mesh):
    placed = (
        P(("groups", "outer", "inner"), None),
        P(("groups", "outer", "inner"), None),
        P(("groups", "outer", "inner"), None),
        P(("groups", "outer", "inner"), None),
        P(("groups", "outer", "inner"), None),
        P(("groups", "outer", "inner"), None),
        P(),
        P(),
    )
    return jax.shard_map(
        local,
        mesh=mesh,
        in_specs=placed,
        out_specs=P(("groups", "outer", "inner"), None),
        check_vma=False,
    )
```

profile of v0, /device:TPU:0, one launch (start us, length us, event | category | flops | bytes accessed | tf_op | source)
XLA Modules:
  0.0 601.0 jit_solution(4477719836671399538)
XLA Ops:
  10.5 2.9 fusion.39
  18.3 2.1 broadcast_multiply_fusion.1
  22.7 2.0 copy.120
  29.2 2.6 copy.125
  32.2 2.3 fusion.44
  38.9 1.8 copy.119
  41.4 74.1 %all-gather.13.cloned.1.call-done = f32[32,128,256]{2,1,0:T(8,128)} async-done(((f32[8,128,256]{2,1,0:T(8,128)}), f32[32,128,256]{2,1,0:T(8,128)}) %all-gather.13.cloned.1.call-update) | async-done | bytes 4194320 | tf_op jit(solution)/shard_map/all_gather | solution.py:9
  115.4 149.8 %all-gather.11.cloned.1.call-done = f32[32,256,256]{2,1,0:T(8,128)} async-done(((f32[8,256,256]{2,1,0:T(8,128)}), f32[32,256,256]{2,1,0:T(8,128)}) %all-gather.11.cloned.1.call-update) | async-done | bytes 8388624 | tf_op jit(solution)/shard_map/all_gather | solution.py:9
  265.4 49.7 %while.30 = (s32[]{:T(128)}, f32[8,256,256]{1,2,0:T(8,128)S(1)}, f32[8,128,256]{1,2,0:T(8,128)}, s32[]{:T(128)}, f32[4,8,256,256]{3,2,1,0:T(8,128)}, /*index=5*/f32[4,8,128,256]{3,2,1,0:T(8,128)}, s32[]{:T(128)}, s32[]{:T(128)}) while((s32[]{:T(128)}, f32[8,256,256]{1,2,0:T(8,128)S(1)}, f32[8,128,256]{1,2,0:T(8,128)}, s32[]{:T(128)}, ...), condition=%wide.region_7.8_spmd.clone, body=%wide.region_6.7_spmd.clone.sunk | while | flops 2417491968 | bytes 25168492 | solution.py:18
  265.4 2.3 constant_dynamic-slice_fusion.5
  270.5 6.1 %fusion.112 = f32[8,128,256]{1,2,0:T(8,128)} fusion(f32[4,8,256,256]{3,2,1,0:T(8,128)} %get-tuple-element.387, s32[]{:T(128)} %get-tuple-element.375, f32[1,8,128,256]{2,3,1,0:T(8,128)S(1)} %copy.193, f32[8,128,256]{1,2,0:T(8,128)S(1)} %copy.218, pred[]{:T(512)S(6)} %compare.3, pred[]{:T(512)S(6)} %lt.44), kind=kOutput, calls=%fused_computation.17.clone.1 | convolution fusion | flops 806354944 | bytes 6293504 | tf_op jit(solution)/shard_map/while/body/eval_jaxpr/hij,hjk->hik/dot_general | solution.py:104
  276.8 5.1 bitcast_select_fusion.2
  281.9 2.3 constant_dynamic-slice_fusion.5
  287.0 6.1 %fusion.112 = f32[8,128,256]{1,2,0:T(8,128)} fusion(f32[4,8,256,256]{3,2,1,0:T(8,128)} %get-tuple-element.387, s32[]{:T(128)} %get-tuple-element.375, f32[1,8,128,256]{2,3,1,0:T(8,128)S(1)} %copy.193, f32[8,128,256]{1,2,0:T(8,128)S(1)} %copy.218, pred[]{:T(512)S(6)} %compare.3, pred[]{:T(512)S(6)} %lt.44), kind=kOutput, calls=%fused_computation.17.clone.1 | convolution fusion | flops 806354944 | bytes 6293504 | tf_op jit(solution)/shard_map/while/body/eval_jaxpr/hij,hjk->hik/dot_general | solution.py:104
  293.3 5.1 bitcast_select_fusion.2
  298.4 2.3 constant_dynamic-slice_fusion.5
  303.5 6.1 %fusion.112 = f32[8,128,256]{1,2,0:T(8,128)} fusion(f32[4,8,256,256]{3,2,1,0:T(8,128)} %get-tuple-element.387, s32[]{:T(128)} %get-tuple-element.375, f32[1,8,128,256]{2,3,1,0:T(8,128)S(1)} %copy.193, f32[8,128,256]{1,2,0:T(8,128)S(1)} %copy.218, pred[]{:T(512)S(6)} %compare.3, pred[]{:T(512)S(6)} %lt.44), kind=kOutput, calls=%fused_computation.17.clone.1 | convolution fusion | flops 806354944 | bytes 6293504 | tf_op jit(solution)/shard_map/while/body/eval_jaxpr/hij,hjk->hik/dot_general | solution.py:104
  309.8 5.1 bitcast_select_fusion.2
  315.1 5.2 fusion.49
  320.3 4.8 select_bitcast_fusion
  325.2 119.8 %all-reduce.3.cloned.1.call-done = (f32[1,8,256,256]{3,2,1,0:T(8,128)}, f32[1,8,128,256]{2,3,1,0:T(8,128)}) async-done(((f32[1,8,256,256]{3,2,1,0:T(8,128)}, f32[1,8,128,256]{2,3,1,0:T(8,128)}), (f32[1,8,256,256]{3,2,1,0:T(8,128)}, f32[1,8,128,256]{2,3,1,0:T(8,128)})) %all-reduce.3.cloned.1.call-update) | async-done | bytes 3145744 | tf_op jit(solution)/shard_map/psum | solution.py:23
  445.0 2.5 copy.133
  452.1 5.1 fusion.66
  458.5 22.6 %all-gather.9.cloned.1.call-done = f32[4,8,128,256]{3,2,1,0:T(8,128)} async-done(((f32[1,8,128,256]{3,2,1,0:T(8,128)}), f32[4,8,128,256]{3,2,1,0:T(8,128)}) %all-gather.9.cloned.1.call-update) | async-done | bytes 4194320 | tf_op jit(solution)/shard_map/all_gather | solution.py:138
  481.2 59.7 %all-gather.7.cloned.1.call-done = f32[4,8,256,256]{3,2,1,0:T(8,128)} async-done(((f32[1,8,256,256]{3,2,1,0:T(8,128)}), f32[4,8,256,256]{3,2,1,0:T(8,128)}) %all-gather.7.cloned.1.call-update) | async-done | bytes 8388624 | tf_op jit(solution)/shard_map/all_gather | solution.py:137
  540.9 41.4 %while.29 = (s32[]{:T(128)}, f32[8,128,256]{1,2,0:T(8,128)}, s32[]{:T(128)}, f32[4,8,256,256]{3,2,1,0:T(8,128)}, f32[4,8,128,256]{3,2,1,0:T(8,128)}, /*index=5*/s32[]{:T(128)}) while((s32[]{:T(128)}, f32[8,128,256]{1,2,0:T(8,128)}, s32[]{:T(128)}, f32[4,8,256,256]{3,2,1,0:T(8,128)}, f32[4,8,128,256]{3,2,1,0:T(8,128)}, ...), condition=%wide.region_11.12_spmd, body=%wide.region_10.11_spmd.sunk | while | flops 805830656 | bytes 16777840 | solution.py:119
  545.3 6.1 %fusion.107 = f32[8,128,256]{1,2,0:T(8,128)} fusion(f32[8,128,256]{1,2,0:T(8,128)S(1)} %copy.216, f32[4,8,256,256]{3,2,1,0:T(8,128)} %get-tuple-element.406, s32[]{:T(128)} %get-tuple-element.397, f32[1,8,128,256]{2,3,1,0:T(8,128)S(1)} %copy-done, pred[]{:T(512)S(6)} %lt.43), kind=kOutput, calls=%fused_computation.5.clone.1 | convolution fusion | flops 805830656 | bytes 6291969 | tf_op jit(solution)/shard_map/while/body/eval_jaxpr/hij,hjk->hik/dot_general | solution.py:104
  555.6 6.1 %fusion.107 = f32[8,128,256]{1,2,0:T(8,128)} fusion(f32[8,128,256]{1,2,0:T(8,128)S(1)} %copy.216, f32[4,8,256,256]{3,2,1,0:T(8,128)} %get-tuple-element.406, s32[]{:T(128)} %get-tuple-element.397, f32[1,8,128,256]{2,3,1,0:T(8,128)S(1)} %copy-done, pred[]{:T(512)S(6)} %lt.43), kind=kOutput, calls=%fused_computation.5.clone.1 | convolution fusion | flops 805830656 | bytes 6291969 | tf_op jit(solution)/shard_map/while/body/eval_jaxpr/hij,hjk->hik/dot_general | solution.py:104
  565.9 6.1 %fusion.107 = f32[8,128,256]{1,2,0:T(8,128)} fusion(f32[8,128,256]{1,2,0:T(8,128)S(1)} %copy.216, f32[4,8,256,256]{3,2,1,0:T(8,128)} %get-tuple-element.406, s32[]{:T(128)} %get-tuple-element.397, f32[1,8,128,256]{2,3,1,0:T(8,128)S(1)} %copy-done, pred[]{:T(512)S(6)} %lt.43), kind=kOutput, calls=%fused_computation.5.clone.1 | convolution fusion | flops 805830656 | bytes 6291969 | tf_op jit(solution)/shard_map/while/body/eval_jaxpr/hij,hjk->hik/dot_general | solution.py:104
  576.2 6.1 %fusion.107 = f32[8,128,256]{1,2,0:T(8,128)} fusion(f32[8,128,256]{1,2,0:T(8,128)S(1)} %copy.216, f32[4,8,256,256]{3,2,1,0:T(8,128)} %get-tuple-element.406, s32[]{:T(128)} %get-tuple-element.397, f32[1,8,128,256]{2,3,1,0:T(8,128)S(1)} %copy-done, pred[]{:T(512)S(6)} %lt.43), kind=kOutput, calls=%fused_computation.5.clone.1 | convolution fusion | flops 805830656 | bytes 6291969 | tf_op jit(solution)/shard_map/while/body/eval_jaxpr/hij,hjk->hik/dot_general | solution.py:104
  582.3 4.0 convolution_add_fusion
  589.4 2.5 fusion.45
  (157 shorter events, 57.5 us)
Async XLA Ops:
  6.5 108.9 %all-gather.13.cloned.1.call-start = ((), (), s32[]{:S(2)}) async-start(), calls=%async_computation.3 | async-start | bytes 5242880 | tf_op jit(solution)/shard_map/all_gather | solution.py:9
  6.6 6.9 %copy-start.25 = (pred[256,256]{1,0:T(8,128)(4,1)}, pred[256,256]{1,0:T(8,128)(4,1)S(1)}, u32[]{:S(2)}) copy-start(pred[256,256]{1,0:T(8,128)(4,1)S(1)} %iota_compare_fusion) | copy-start | bytes 196612
  8.2 5.3 copy-start.28
  10.5 3.0 copy-start.31
  10.5 3.0 copy-start.27
  10.5 4.4 copy-start.21
  18.3 2.1 copy-start.23
  20.4 16.1 %copy-start.2 = (f32[256,8,128]{2,1,0:T(8,128)}, f32[256,8,128]{2,1,0:T(8,128)S(1)}, u32[]{:S(2)}) copy-start(f32[256,8,128]{2,1,0:T(8,128)S(1)} %get-tuple-element.291) | copy-start | bytes 3145732
  24.8 1.7 copy-start.6
  29.2 3.0 copy-start.32
  29.2 3.0 copy-start.26
  29.2 3.0 copy-start.29
  29.2 3.0 copy-start.30
  31.8 233.4 %all-gather.11.cloned.1.call-start = ((), (), s32[]{:S(2)}) async-start(), calls=%async_computation.2 | async-start | bytes 10485760 | tf_op jit(solution)/shard_map/all_gather | solution.py:9
  35.1 2.9 copy-start.8
  35.1 2.9 copy-start.10
  40.7 404.2 %all-reduce.3.cloned.1.call-start = ((), (), s32[]{:S(2)}) async-start(), calls=%async_computation.4 | async-start | bytes 6291456 | tf_op jit(solution)/shard_map/psum | solution.py:23
  315.1 5.2 copy-start.9
  315.1 5.2 copy-start.11
  315.1 5.2 copy-start.13
  315.1 5.2 copy-start.15
  325.2 156.0 %all-gather.9.cloned.1.call-start = ((), (), s32[]{:S(2)}) async-start(), calls=%async_computation.1 | async-start | bytes 5242880 | tf_op jit(solution)/shard_map/all_gather | solution.py:138
  447.5 2.0 copy-start.24
  447.5 93.4 %all-gather.7.cloned.1.call-start = ((), (), s32[]{:S(2)}) async-start(), calls=%async_computation | async-start | bytes 10485760 | tf_op jit(solution)/shard_map/all_gather | solution.py:137
  452.1 5.1 copy-start.1
  543.8 1.5 copy-start
  554.1 1.5 copy-start
  564.4 1.5 copy-start
  574.7 1.5 copy-start
  582.3 4.0 copy-start.4
  586.3 2.5 copy-start.17
  587.6 1.7 copy-start.5
  (9 other events, 9.9 us)
Sparse Core Ops, SparseCore 0:
  31.9 83.4 all-gather.12
  117.0 148.1 all-gather.10
  325.3 119.6 all-reduce.2
  447.7 33.4 all-gather.8
  482.6 58.2 all-gather.6
where the time goes:
time: 609 us; the launch traced here: 601 us
  waiting for transfers between devices  427 us (70%)
  matrix products  93.8 us (15%)
  local copies, waits for them, and re-layouts  56.5 us (9%)
  between operations  13.9 us (2%)
  other arithmetic  8.6 us (1%)
    all_gather x2, waiting for transfers between devices, carried_in(): pieces = jax.tree.map(lambda part: lax.all_gather(part, axis), value)  224 us
    psum x1, waiting for transfers between devices, from_root(): return lax.psum(block, axis)  120 us
    all_gather x1, waiting for transfers between devices, local(): lax.all_gather(group_map[0][None], 'outer', axis=0, tiled=True)  59.7 us
    dot_general x9, matrix products, advance_state(): jnp.einsum('hij,hjk->hik', carried, transition, precision=lax.Precision.H...  51.8 us
    all_gather x1, waiting for transfers between devices, local(): lax.all_gather(group_map[1][None], 'outer', axis=0, tiled=True)  22.6 us
    dot_general x4, matrix products, compose(): jnp.einsum('hij,hjk->hik', earlier[0], later[0], precision=lax.Precision....  20.2 us
  transfers between devices with their start and end apart: 5, of which 5 were waited for; matrix products, arithmetic and copies ran while one was open for 3% of the time, Pallas kernels for 0%

commit v1 on v0

--- a/solution.py
+++ b/solution.py
@@ -1,7 +1,28 @@
+import functools
 import jax
 import jax.numpy as jnp
 from jax import lax
 from jax.sharding import PartitionSpec as P
+
+
+def lay_node(packet, ax_name):
+    current_block = lax.axis_size(ax_name)
+    inter = lax.axis_index(ax_name)
+    v_now, opened = (current_block, inter)
+    odd, heard = (packet, 1)
+    while heard < v_now:
+        views = []
+        for rr in range(v_now):
+            views.append((rr, rr ^ heard))
+        carry_out = lax.ppermute(odd, ax_name, views)
+        then = jnp.concatenate([odd, carry_out], axis=0)
+        upper = jnp.concatenate([carry_out, odd], axis=0)
+        odd = jnp.where(opened & heard == 0, then, upper)
+        heard = 2 * heard
+    return odd
+
+
+domain_open = functools.partial(lay_node, ax_name="outer")
 
 
 def carried_in(value, axis, join, neutral):
@@ -134,7 +155,7 @@
         from_root(through[1], "inner", last_inner),
     )
     gathered = (
-        lax.all_gather(group_map[0][None], "outer", axis=0, tiled=True),
+        domain_open(group_map[0][None]),
         lax.all_gather(group_map[1][None], "outer", axis=0, tiled=True),
     )
     entry_state = apply_earlier(gathered, first_state)

time: 609 us -> 647 us (1.062)
  waiting for transfers between devices: 427 us -> 448 us
  other arithmetic: 8.6 us -> 24.4 us
    ppermute x0 -> x2, waiting for transfers between devices: none -> 105 us  [lay_node(): carry_out = lax.ppermute(odd, ax_name, views)]
    all_gather x1 -> x0, waiting for transfers between devices: 59.7 us -> none  [local(): lax.all_gather(group_map[0][None], 'outer', axis=0, tiled=True)]
    all_gather x1, waiting for transfers between devices: 22.6 us -> 0.01 us  [local(): lax.all_gather(group_map[1][None], 'outer', axis=0, tiled=True)]
    select_n x0 -> x2, other arithmetic: none -> 16.4 us  [lay_node(): odd = jnp.where(opened & heard == 0, then, upper)]
  transfers between devices with their start and end apart: 5 -> 6, of which waited for: 5 -> 5; matrix products, arithmetic and copies ran while one was open for 3% -> 6% of each run, Pallas kernels for 0% -> 0%
where the time goes in v1:
time: 647 us; the launch traced here: 639 us
  waiting for transfers between devices  448 us (69%)
  matrix products  93.8 us (14%)
  local copies, waits for them, and re-layouts  56.1 us (9%)
  other arithmetic  24.4 us (4%)
  between operations  14 us (2%)
    all_gather x2, waiting for transfers between devices, carried_in(): pieces = jax.tree.map(lambda part: lax.all_gather(part, axis), value)  224 us
    psum x1, waiting for transfers between devices, from_root(): return lax.psum(block, axis)  120 us
    ppermute x2, waiting for transfers between devices, lay_node(): carry_out = lax.ppermute(odd, ax_name, views)  105 us
    dot_general x9, matrix products, advance_state(): jnp.einsum('hij,hjk->hik', carried, transition, precision=lax.Precision.H...  51.9 us
    dot_general x4, matrix products, compose(): jnp.einsum('hij,hjk->hik', earlier[0], later[0], precision=lax.Precision....  20.2 us
    select_n x2, other arithmetic, lay_node(): odd = jnp.where(opened & heard == 0, then, upper)  16.4 us
  transfers between devices with their start and end apart: 6, of which 5 were waited for; matrix products, arithmetic and copies ran while one was open for 6% of the time, Pallas kernels for 0%

profile of v1, /device:TPU:0, one launch (start us, length us, event | category | flops | bytes accessed | tf_op | source)
XLA Modules:
  0.0 639.3 jit_solution(9182630735441655606)
XLA Ops:
  10.5 2.9 fusion.39
  17.7 2.1 broadcast_multiply_fusion.1
  22.1 2.0 copy.120
  28.7 2.6 copy.125
  31.6 2.3 fusion.44
  40.8 74.1 %all-gather.10.cloned.1.call-done = f32[32,128,256]{2,1,0:T(8,128)} async-done(((f32[8,128,256]{2,1,0:T(8,128)}), f32[32,128,256]{2,1,0:T(8,128)}) %all-gather.10.cloned.1.call-update) | async-done | bytes 4194320 | tf_op jit(solution)/shard_map/all_gather | solution.py:30
  114.9 149.8 %all-gather.8.cloned.1.call-done = f32[32,256,256]{2,1,0:T(8,128)} async-done(((f32[8,256,256]{2,1,0:T(8,128)}), f32[32,256,256]{2,1,0:T(8,128)}) %all-gather.8.cloned.1.call-update) | async-done | bytes 8388624 | tf_op jit(solution)/shard_map/all_gather | solution.py:30
  264.8 49.5 %while.30 = (s32[]{:T(128)}, f32[8,256,256]{1,2,0:T(8,128)S(1)}, f32[8,128,256]{1,2,0:T(8,128)}, s32[]{:T(128)}, f32[4,8,256,256]{3,2,1,0:T(8,128)}, /*index=5*/f32[4,8,128,256]{3,2,1,0:T(8,128)}, s32[]{:T(128)}, s32[]{:T(128)}) while((s32[]{:T(128)}, f32[8,256,256]{1,2,0:T(8,128)S(1)}, f32[8,128,256]{1,2,0:T(8,128)}, s32[]{:T(128)}, ...), condition=%wide.region_7.8_spmd.clone, body=%wide.region_6.7_spmd.clone.sunk | while | flops 2417491968 | bytes 25168492 | solution.py:39
  264.8 2.3 constant_dynamic-slice_fusion.5
  269.9 6.1 fusion.112
  276.1 5.1 bitcast_select_fusion.2
  281.3 2.3 constant_dynamic-slice_fusion.5
  286.3 6.1 fusion.112
  292.6 5.1 bitcast_select_fusion.2
  297.7 2.3 constant_dynamic-slice_fusion.5
  302.8 6.1 fusion.112
  309.0 5.1 bitcast_select_fusion.2
  314.4 5.2 fusion.49
  319.5 4.8 select_bitcast_fusion
  324.4 119.8 %all-reduce.3.cloned.1.call-done = (f32[1,8,256,256]{3,2,1,0:T(8,128)}, f32[1,8,128,256]{2,3,1,0:T(8,128)}) async-done(((f32[1,8,256,256]{3,2,1,0:T(8,128)}, f32[1,8,128,256]{2,3,1,0:T(8,128)}), (f32[1,8,256,256]{3,2,1,0:T(8,128)}, f32[1,8,128,256]{2,3,1,0:T(8,128)})) %all-reduce.3.cloned.1.call-update) | async-done | bytes 3145744 | tf_op jit(solution)/shard_map/psum | solution.py:44
  444.2 2.6 copy.133
  448.7 6.2 maximum_select_fusion.1
  459.8 5.0 fusion.66
  466.1 102.9 %collective-permute-done.1 = f32[2,8,256,256]{3,2,1,0:T(8,128)} collective-permute-done((f32[2,8,256,256]{3,2,1,0:T(8,128)}, f32[2,8,256,256]{3,2,1,0:T(8,128)}, u32[]{:S(2)}, u32[]{:S(2)}) %collective-permute-start.1) | collective-permute-done | bytes 4194336 | tf_op jit(solution)/shard_map/ppermute | solution.py:17
  568.9 10.2 %maximum_select_fusion = f32[4,8,256,256]{3,2,1,0:T(8,128)} fusion(f32[2,8,256,256]{3,2,1,0:T(8,128)} %collective-permute-done.1, f32[2,8,256,256]{3,2,1,0:T(8,128)} %maximum_select_fusion.1, pred[]{:T(512)S(6)} %eq.24), kind=kLoop, calls=%fused_computation.25 | loop fusion | flops 6291456 | bytes 16777216 | tf_op jit(solution)/shard_map/jit(_where)/select_n | solution.py:20
  579.2 41.4 %while.29 = (s32[]{:T(128)}, f32[8,128,256]{1,2,0:T(8,128)}, s32[]{:T(128)}, f32[4,8,256,256]{3,2,1,0:T(8,128)}, f32[4,8,128,256]{3,2,1,0:T(8,128)}, /*index=5*/s32[]{:T(128)}) while((s32[]{:T(128)}, f32[8,128,256]{1,2,0:T(8,128)}, s32[]{:T(128)}, f32[4,8,256,256]{3,2,1,0:T(8,128)}, f32[4,8,128,256]{3,2,1,0:T(8,128)}, ...), condition=%wide.region_11.12_spmd, body=%wide.region_10.11_spmd.sunk | while | flops 805830656 | bytes 16777840 | solution.py:140
  583.4 6.1 fusion.107
  593.7 6.1 fusion.107
  604.1 6.1 fusion.107
  614.4 6.1 fusion.107
  620.6 4.0 convolution_add_fusion
  627.6 2.6 fusion.45
  (160 shorter events, 61.1 us)
Async XLA Ops:
  6.5 108.3 %all-gather.10.cloned.1.call-start = ((), (), s32[]{:S(2)}) async-start(), calls=%async_computation.2 | async-start | bytes 5242880 | tf_op jit(solution)/shard_map/all_gather | solution.py:30
  6.6 6.9 %copy-start.25 = (pred[256,256]{1,0:T(8,128)(4,1)}, pred[256,256]{1,0:T(8,128)(4,1)S(1)}, u32[]{:S(2)}) copy-start(pred[256,256]{1,0:T(8,128)(4,1)S(1)} %iota_compare_fusion) | copy-start | bytes 196612
  8.2 5.3 copy-start.28
  10.5 4.3 copy-start.31
  10.5 4.3 copy-start.27
  10.5 4.6 copy-start.21
  17.7 2.1 copy-start.23
  19.8 16.1 %copy-start.2 = (f32[256,8,128]{2,1,0:T(8,128)}, f32[256,8,128]{2,1,0:T(8,128)S(1)}, u32[]{:S(2)}) copy-start(f32[256,8,128]{2,1,0:T(8,128)S(1)} %get-tuple-element.291) | copy-start | bytes 3145732
  24.2 1.7 copy-start.6
  28.7 2.9 copy-start.32
  28.7 3.0 copy-start.26
  28.7 3.0 copy-start.29
  28.7 3.0 copy-start.30
  31.3 233.4 %all-gather.8.cloned.1.call-start = ((), (), s32[]{:S(2)}) async-start(), calls=%async_computation.1 | async-start | bytes 10485760 | tf_op jit(solution)/shard_map/all_gather | solution.py:30
  34.5 2.9 copy-start.8
  34.5 2.9 copy-start.10
  40.2 404.0 %all-reduce.3.cloned.1.call-start = ((), (), s32[]{:S(2)}) async-start(), calls=%async_computation.3 | async-start | bytes 6291456 | tf_op jit(solution)/shard_map/psum | solution.py:44
  314.3 5.2 copy-start.9
  314.3 5.2 copy-start.11
  314.4 5.2 copy-start.13
  314.4 5.2 copy-start.15
  324.4 254.8 %all-gather.6.cloned.1.call-start = ((), (), s32[]{:S(2)}) async-start(), calls=%async_computation | async-start | bytes 5242880 | tf_op jit(solution)/shard_map/all_gather | solution.py:159
  444.2 4.5 collective-permute-start
  446.8 9.4 %copy-start.7 = (bf16[256,1024]{0,1:T(8,128)(2,1)S(1)}, bf16[256,1024]{0,1:T(8,128)(2,1)}, u32[]{:S(2)}) copy-start(bf16[256,1024]{0,1:T(8,128)(2,1)} %copy.120) | copy-start | bytes 1572868
  446.8 10.4 %copy-start.24 = (f32[8,128,128]{2,1,0:T(8,128)S(1)}, f32[8,128,128]{2,1,0:T(8,128)}, u32[]{:S(2)}) copy-start(f32[8,128,128]{2,1,0:T(8,128)} %param.18) | copy-start | bytes 1572868
  454.9 114.0 %collective-permute-start.1 = (f32[2,8,256,256]{3,2,1,0:T(8,128)}, f32[2,8,256,256]{3,2,1,0:T(8,128)}, u32[]{:S(2)}, u32[]{:S(2)}) collective-permute-start(f32[2,8,256,256]{3,2,1,0:T(8,128)} %maximum_select_fusion.1), channel_id=1, source_target_pairs={{0,2},{1,3},{2,0},{3,1},{4,6},{5,7},{6,4},{7,5},{8,10},{9,11},{10,... | collective-permute-start | bytes 12582920 | tf_op jit(solution)/shard_map/ppermute | solution.py:17
  459.7 5.0 copy-start.1
  581.8 1.5 copy-start
  592.2 1.5 copy-start
  620.6 4.0 copy-start.4
  624.6 2.5 copy-start.17
  625.9 1.7 copy-start.5
  (10 other events, 11.9 us)
Sparse Core Ops, SparseCore 0:
  31.4 83.4 all-gather.9
  116.4 148.1 all-gather.7
  324.5 119.6 all-reduce.2
  446.9 54.9 all-gather.5
